TPU v7x, 32 devices: a whole 2x2x4 slice. The times are simulated.
32 devices in a mesh: groups: 2 (over x), wide: 8 (over z, y), narrow: 2 (over core).
Axes of the slice: x: 2, y: 2, z: 4, core: 2. Of those that a mesh axis runs over, the one named last changes fastest.
Arguments:
- context_symbol_ids: int32 [2, 16, 16], P('narrow', 'groups'), parts along dimension 1, may hold values from 0 to 32767
- context_symbol_spans: int32 [2, 16], P('narrow', 'groups'), parts along dimension 1, may hold values from 1 to 16, as said below
- symbol_vector_lookup: bfloat16 [4096, 32768], P('wide'), may hold values from -6 to 6
- opening_lagged_blend: float32 [4096], replicated, may hold values from 0 to 1
- lagged_blend_weights: float32 [3, 4096], replicated, may hold values from 0 to 1
- blending_left_operand: bfloat16 [4096, 192], replicated, may hold values from -0.09375 to 0.09375
- blending_right_operands: bfloat16 [3, 64, 4096], replicated, may hold values from -0.375 to 0.375
- fixed_fading_scores: float32 [4096], P('wide'), may hold values from -6 to -1
- fading_left_operand: bfloat16 [4096, 128], replicated, may hold values from -0.09375 to 0.09375
- fading_right_operand: bfloat16 [128, 4096], P(None, 'wide'), may hold values from -0.5 to 0.5
- address_projector: bfloat16 [4096, 4096], P('wide'), may hold values from -0.09375 to 0.09375
- payload_projector: bfloat16 [4096, 4096], P('wide'), may hold values from -0.09375 to 0.09375
- present_symbol_reward: float32 [64, 64], replicated, may hold values from -1 to 1
- cluster_scaling_weight: float32 [4096], replicated, may hold values from 0.5 to 1.5
- cluster_scaling_offset: float32 [4096], replicated, may hold values from -3 to 3
- generated_acceptance: bfloat16 [2, 16, 4, 4096], P(None, ('groups', 'wide'), None, 'narrow'), parts along dimension 1, may hold values from -6 to 6
- generated_addresses: bfloat16 [2, 16, 4, 4096], P(None, ('groups', 'wide'), None, 'narrow'), parts along dimension 1, may hold values from -6 to 6
- generated_payloads: bfloat16 [2, 16, 4, 4096], P(None, ('groups', 'wide'), None, 'narrow'), parts along dimension 1, may hold values from -6 to 6
- generated_fading_scores: bfloat16 [2, 16, 4, 4096], P(None, ('groups', 'wide'), None, 'narrow'), parts along dimension 1, may hold values from -6 to -1
- generated_valve_scores: bfloat16 [2, 16, 4, 4096], P(None, ('groups', 'wide'), None, 'narrow'), parts along dimension 1, may hold values from -6 to 6
Outputs:
- dec_out: bfloat16 [2, 16, 4, 4096], P(None, ('groups', 'wide'), None, 'narrow'), parts along dimension 1
There are 2 independent parts, one for each index of `groups`. A program takes and returns all parts, laid end to end along the dimension named above; an argument that names none is the same for every part. Nothing has to cross between parts.
Inputs may be any that keep to these rules, and one draw needn't show every extreme that they name: `context_symbol_spans`: positions at or past a prompt's length are padding. In every draw one of the 2 banks, chosen by the draw, holds only prompts of exactly 16 tokens, and every other bank holds at least one prompt of 16 tokens.
All inputs are finite; a program needn't handle non-finite values.
Results may differ from a plain program's by a relative error of at most 0.0095.
Values may be sent and summed in bfloat16 or wider, within the bound.
No kernel may reach another device: no remote copies, remote signals or barrier semaphores. Data moves between devices by JAX's collectives and lax.ppermute only.
A program may use at most 128 MiB of HBM per device.

v0:
```python
import jax
import jax.numpy as jnp
from jax import lax
from jax.sharding import PartitionSpec as P

norm_eps = 0.00064


def mix_project(
    embedded,
    opening_lagged_blend,
    lagged_blend_weights,
    blending_left_operand,
    blending_right_operands,
    fixed_fading_scores,
    fading_left_operand,
    fading_right_operand,
    address_projector,
    payload_projector,
):
    features = embedded.shape[2]
    previous = jnp.pad(embedded, ((0, 0), (1, 0), (0, 0)))[:, :-1, :]
    current = embedded.reshape(-1, features).astype(jnp.float32)
    difference = previous.reshape(-1, features).astype(jnp.float32) - current
    mixed_in = (current + difference * opening_lagged_blend).astype(jnp.bfloat16)
    hidden = jnp.tanh(
        jnp.dot(mixed_in, blending_left_operand, preferred_element_type=jnp.float32)
    ).astype(jnp.bfloat16)
    rank_size = blending_right_operands.shape[1]
    branches = []
    for branch in range(3):
        shift_term = jnp.dot(
            hidden[:, branch * rank_size : (branch + 1) * rank_size],
            blending_right_operands[branch],
            preferred_element_type=jnp.float32,
        )
        branches.append(
            (current + difference * (lagged_blend_weights[branch] + shift_term)).astype(
                jnp.bfloat16
            )
        )
    decay_hidden = jnp.tanh(
        jnp.dot(branches[0], fading_left_operand, preferred_element_type=jnp.float32)
    ).astype(jnp.bfloat16)
    decay_log = fixed_fading_scores + jnp.dot(
        decay_hidden, fading_right_operand, preferred_element_type=jnp.float32
    )
    key_proj = jnp.dot(branches[1], address_projector.T, preferred_element_type=jnp.float32).astype(
        jnp.bfloat16
    )
    value_proj = jnp.dot(
        branches[2], payload_projector.T, preferred_element_type=jnp.float32
    ).astype(jnp.bfloat16)
    return (key_proj, value_proj, decay_log)


def final_states(key_proj, value_proj, decay_log, lengths, attender_width):
    bank_rows, length, columns = key_proj.shape
    attender_ordinal = columns // attender_width
    decay_rates = jnp.exp(decay_log)
    places = lax.broadcasted_iota(jnp.int32, (bank_rows, length), 1)
    live_mask = (places < lengths[:, None])[:, :, None]
    running = jnp.cumsum(jnp.where(live_mask, decay_rates, 0.0), axis=1)
    remaining = running[:, -1:, :] - running
    weights = jnp.where(live_mask, jnp.exp(-remaining), 0.0)
    weighted = (key_proj.astype(jnp.float32) * weights).reshape(
        bank_rows, length, attender_ordinal, attender_width
    )
    plain_values = value_proj.astype(jnp.float32).reshape(
        bank_rows, length, attender_ordinal, attender_width
    )
    return jnp.einsum("rlhi,rlhj->rhij", weighted, plain_values, precision=lax.Precision.HIGHEST)


def generation_iterations(
    recurrent_memories,
    acceptance_lines,
    address_source,
    payload_source,
    fading_source,
    valve_source,
    shard_reward,
    shard_scaling_weight,
    shard_scaling_offset,
):
    attender_ordinal = recurrent_memories.shape[-3]
    attender_width = recurrent_memories.shape[-1]
    leading = acceptance_lines.shape[:-2]
    step_count = acceptance_lines.shape[-2]
    split_shape = leading + (step_count, attender_ordinal, attender_width)
    receptance = acceptance_lines.astype(jnp.float32).reshape(split_shape)
    key_split = address_source.astype(jnp.float32).reshape(split_shape)
    valued = payload_source.astype(jnp.float32).reshape(split_shape)
    factors = jnp.exp(-jnp.exp(fading_source.astype(jnp.float32))).reshape(split_shape)
    results = []
    for position in range(step_count):
        present_acceptance = receptance[..., position, :, :]
        present_address = key_split[..., position, :, :]
        present_payload = valued[..., position, :, :]
        immediate_summand = (
            jnp.sum(present_acceptance * shard_reward * present_address, axis=-1, keepdims=True)
            * present_payload
        )
        carried = jnp.einsum(
            "...hi,...hij->...hj",
            present_acceptance,
            recurrent_memories,
            precision=lax.Precision.HIGHEST,
        )
        results.append(carried + immediate_summand)
        if position + 1 < step_count:
            recurrent_memories = (
                factors[..., position, :, :][..., :, None] * recurrent_memories
                + present_address[..., :, None] * present_payload[..., None, :]
            )
    mixed_out = jnp.stack(results, axis=-3)
    average = jnp.mean(mixed_out, axis=-1, keepdims=True)
    centred = mixed_out - average
    spread = jnp.mean(centred * centred, axis=-1, keepdims=True)
    normed = (centred * lax.rsqrt(spread + norm_eps)).reshape(
        leading + (step_count, attender_ordinal * attender_width)
    )
    return (
        (normed * shard_scaling_weight + shard_scaling_offset)
        * jax.nn.silu(valve_source.astype(jnp.float32))
    ).astype(jnp.bfloat16)


def per_device(
    context_symbol_ids,
    context_symbol_spans,
    symbol_vector_lookup,
    opening_lagged_blend,
    lagged_blend_weights,
    blending_left_operand,
    blending_right_operands,
    fixed_fading_scores,
    fading_left_operand,
    fading_right_operand,
    address_projector,
    payload_projector,
    present_symbol_reward,
    cluster_scaling_weight,
    cluster_scaling_offset,
    generated_acceptance,
    generated_addresses,
    generated_payloads,
    generated_fading_scores,
    generated_valve_scores,
):
    bank_rows = context_symbol_ids.shape[1]
    length = context_symbol_ids.shape[2]
    columns = symbol_vector_lookup.shape[0]
    attender_width = present_symbol_reward.shape[1]
    head_local = columns // attender_width
    lengths = context_symbol_spans.reshape(-1)
    picked = jnp.take(symbol_vector_lookup, context_symbol_ids.reshape(-1), axis=1)
    gathered = lax.all_gather(picked, "wide", axis=0, tiled=True).T
    features = gathered.shape[1]
    block_rows = bank_rows
    while block_rows % 2 == 0 and block_rows * length > 1024:
        block_rows = block_rows // 2
    blocks = gathered.reshape(bank_rows // block_rows, block_rows, length, features)
    length_blocks = lengths.reshape(bank_rows // block_rows, block_rows)

    def one_block(block_item):
        key_proj, value_proj, decay_log = mix_project(
            block_item[0],
            opening_lagged_blend,
            lagged_blend_weights,
            blending_left_operand,
            blending_right_operands,
            fixed_fading_scores,
            fading_left_operand,
            fading_right_operand,
            address_projector,
            payload_projector,
        )
        block_shape = (block_rows, length, columns)
        return final_states(
            key_proj.reshape(block_shape),
            value_proj.reshape(block_shape),
            decay_log.reshape(block_shape),
            block_item[1],
            attender_width,
        )

    recurrent_memories = lax.map(one_block, (blocks, length_blocks)).reshape(
        bank_rows, head_local, attender_width, attender_width
    )
    handed = lax.all_to_all(
        lax.all_to_all(
            recurrent_memories.reshape(1, bank_rows, head_local, attender_width * attender_width),
            "wide",
            split_axis=1,
            concat_axis=2,
            tiled=True,
        ),
        "narrow",
        split_axis=2,
        concat_axis=0,
        tiled=True,
    )
    generated_by_attender = handed.shape[2]
    leading_attender_offset = lax.axis_index("narrow") * generated_by_attender
    shard_reward = lax.dynamic_slice_in_dim(
        present_symbol_reward, leading_attender_offset, generated_by_attender, 0
    )
    shard_scaling_weight = lax.dynamic_slice_in_dim(
        cluster_scaling_weight,
        leading_attender_offset * attender_width,
        generated_by_attender * attender_width,
        0,
    )
    shard_scaling_offset = lax.dynamic_slice_in_dim(
        cluster_scaling_offset,
        leading_attender_offset * attender_width,
        generated_by_attender * attender_width,
        0,
    )
    result = generation_iterations(
        handed.reshape(handed.shape[:3] + (attender_width, attender_width)),
        generated_acceptance,
        generated_addresses,
        generated_payloads,
        generated_fading_scores,
        generated_valve_scores,
        shard_reward,
        shard_scaling_weight,
        shard_scaling_offset,
    )
    return result


def solution(mesh):
    placed = (
        P("narrow", "groups", None),
        P("narrow", "groups"),
        P("wide", None),
        P(),
        P(),
        P(),
        P(),
        P("wide"),
        P(),
        P(None, "wide"),
        P("wide", None),
        P("wide", None),
        P(),
        P(),
        P(),
        P(None, ("groups", "wide"), None, "narrow"),
        P(None, ("groups", "wide"), None, "narrow"),
        P(None, ("groups", "wide"), None, "narrow"),
        P(None, ("groups", "wide"), None, "narrow"),
        P(None, ("groups", "wide"), None, "narrow"),
    )
    return jax.shard_map(
        per_device,
        mesh=mesh,
        in_specs=placed,
        out_specs=P(None, ("groups", "wide"), None, "narrow"),
        check_vma=False,
    )
```

profile of v0, /device:TPU:0, one launch (start us, length us, event | category | flops | bytes accessed | tf_op | source)
XLA Modules:
  0.0 180.6 jit_solution(2919527989202924769)
XLA Ops:
  6.5 0.9 reshape.534
  7.4 0.8 reshape.533
  8.2 44.0 %copy.70 = bf16[512,32768]{0,1:T(8,128)(2,1)} copy(bf16[512,32768]{1,0:T(8,128)(2,1)} %param.22) | data formatting | bytes 67108864 | tf_op args[2]
  52.2 2.0 %gather_fusion = bf16[128,512]{1,0:T(8,128)(2,1)S(1)} fusion(bf16[512,32768]{0,1:T(8,128)(2,1)} %copy.70, s32[1024]{0:T(1024)S(1)} %pad_clamp_fusion), kind=kCustom, calls=%fused_computation | custom fusion | bytes 262656 | tf_op jit(solution)/shard_map/jit(_take)/gather | solution.py:157
  54.2 0.7 select_bitcast_fusion
  55.1 42.1 %all-gather.2.cloned.1.call-done = bf16[4096,128]{0,1:T(8,128)(2,1)} async-done(((bf16[512,128]{0,1:T(8,128)(2,1)}), bf16[4096,128]{0,1:T(8,128)(2,1)}) %all-gather.2.cloned.1.call-update) | async-done | bytes 1048592 | tf_op jit(solution)/shard_map/all_gather | solution.py:158
  97.2 1.6 pad_slice_fusion
  98.8 0.7 fusion.20
  99.8 2.7 %fusion.22 = bf16[128,128]{1,0:T(8,128)(2,1)S(1)} fusion(bf16[4096,128]{1,0:T(8,128)(2,1)} %param.28, bf16[128,4096]{1,0:T(8,128)(2,1)} %bitcast.181, bf16[4096,128]{0,1:T(8,128)(2,1)S(1)} %copy-done.3, f32[4096]{0:T(1024)S(1)} %bitcast.199, bf16[3,64,4096]{2,1,0:T(8,128)(2,1)} %param.26, bf16[128,192]{0,1:T(8,128)(2,1)S(1)} %fusion.20), kind=kOutput, calls=%fused_computation.35 | convolution fusion | flops 205012992 | bytes 3735552 | tf_op jit(solution)/shard_map/while/body/eval_jaxpr/dot_general | solution.py:43
  103.1 4.7 %convolution_convert_fusion = bf16[128,512]{1,0:T(8,128)(2,1)S(1)} fusion(bf16[512,4096]{1,0:T(8,128)(2,1)} %param.31, bf16[128,4096]{1,0:T(8,128)(2,1)} %bitcast.182, bf16[4096,128]{0,1:T(8,128)(2,1)S(1)} %copy-done.3, f32[4096]{0:T(1024)S(1)} %bitcast.198, bf16[3,64,4096]{2,1,0:T(8,128)(2,1)} %param.26, bf16[128,192]{0,1:T(8,128)(2,1)S(1)} %fusion.20), kind=kOutput, calls=%fused_computation.29 | convolution fusion | flops 607715328 | bytes 6979584 | tf_op jit(solution)/shard_map/while/body/eval_jaxpr/dot_general | solution.py:51
  108.0 4.7 %fusion.19 = f32[128,512]{1,0:T(8,128)S(1)} fusion(bf16[512,4096]{1,0:T(8,128)(2,1)} %param.30, bf16[128,4096]{1,0:T(8,128)(2,1)} %bitcast.183, bf16[4096,128]{0,1:T(8,128)(2,1)S(1)} %copy-done.3, f32[4096]{0:T(1024)S(1)} %bitcast.197, bf16[3,64,4096]{2,1,0:T(8,128)(2,1)} %param.26, bf16[128,192]{0,1:T(8,128)(2,1)S(1)} %fusion.20), kind=kOutput, calls=%fused_computation.31 | convolution fusion | flops 607780864 | bytes 7110656 | tf_op jit(solution)/shard_map/while/body/eval_jaxpr/dot_general | solution.py:48
  112.8 3.3 %fusion.56 = f32[8,8,64,64]{3,2,1,0:T(8,128)} fusion(f32[8,16,8,64]{3,2,1,0:T(8,128)S(1)} %reshape.549, f32[8,16,8,64]{3,2,0,1:T(8,128)S(1)} %reduce_window_sum.15, bf16[8,16,8,64]{3,2,1,0:T(8,128)(2,1)S(1)} %reshape.535, f32[8,8,64]{2,1,0:T(8,128)S(1)} %sub.51, pred[8,16]{1,0:T(8,128)(4,1)S(1)} %copy.71), kind=kOutput, calls=%fused_computation.66 | convolution fusion | flops 50593792 | bytes 1720448 | tf_op jit(solution)/shard_map/while/body/eval_jaxpr/rlhi,rlhj->rhij/dot_general | solution.py:72
  116.1 2.9 %reshape_reshape.3 = f32[1,8,8,4096]{3,2,1,0:T(8,128)} reshape(f32[8,8,64,64]{3,2,1,0:T(8,128)} %fusion.56) | data formatting | bytes 2097152 | tf_op jit(solution)/shard_map/reshape;reshape | solution.py:193
  119.1 3.7 %all-to-all-start = ((f32[1,8,8,4096]{3,2,0,1:T(8,128)}), f32[1,8,8,4096]{3,2,0,1:T(8,128)S(1)}, u32[]{:S(2)}, u32[]{:S(2)}) async-start(f32[1,8,8,4096]{3,2,0,1:T(8,128)} %bitcast.13), calls=%async_computation | async-start | bytes 2097152 | tf_op jit(solution)/shard_map/all_to_all | solution.py:192
  123.6 23.9 %all-to-all-done = f32[1,8,8,4096]{3,2,0,1:T(8,128)S(1)} async-done(((f32[1,8,8,4096]{3,2,0,1:T(8,128)}), f32[1,8,8,4096]{3,2,0,1:T(8,128)S(1)}, u32[]{:S(2)}, u32[]{:S(2)}) %all-to-all-start) | async-done | bytes 1048608 | tf_op jit(solution)/shard_map/all_to_all | solution.py:192
  147.5 1.1 copy.77
  148.6 4.6 %all_to_all.21 = f32[1,1,64,4096]{3,1,0,2:T(1,128)S(1)} all-to-all(f32[1,1,64,4096]{3,1,0,2:T(1,128)S(1)} %copy.77), channel_id=1, replica_groups=mesh['groups'=2,'wide'=8,'narrow'=2] {'narrow'}, dimensions={2} | all-to-all | bytes 2097152 | tf_op jit(solution)/shard_map/all_to_all | solution.py:191
  153.1 2.6 %reduce.6 = f32[64,4096]{1,0:T(8,128)S(1)} reduce(f32[1,1,64,4096]{3,1,0,2:T(1,128)S(1)} %all_to_all.21, f32[]{:T(128)} %constant.68), dimensions={0,1}, to_apply=%all_to_all.8.reduce_sub_computation | reduce | bytes 2097156 | tf_op jit(solution)/shard_map/all_to_all | solution.py:191
  155.8 2.2 %reshape.536 = f32[2,32,64,64]{3,2,1,0:T(8,128)} reshape(f32[64,4096]{1,0:T(8,128)S(1)} %reduce.6) | data formatting | bytes 2097152 | tf_op jit(solution)/shard_map/reshape.34
  158.0 2.8 %fusion.99 = f32[2,32,1,64]{3,2,1,0:T(1,128)S(1)} fusion(f32[2,32,64,64]{3,2,1,0:T(8,128)} %reshape.536, bf16[2,32,64,1]{2,1,0,3:T(8,128)(2,1)S(1)} %get-tuple-element.61), kind=kOutput, calls=%fused_computation.127 | convolution fusion | flops 3145728 | bytes 1073152 | tf_op jit(solution)/shard_map/...hi,...hij->...hj/dot_general | solution.py:104
  160.8 2.0 %fusion.15 = f32[2,32,1,64]{3,2,1,0:T(1,128)S(1)} fusion(f32[2,32,64,64]{3,2,1,0:T(8,128)S(1)} %copy-done.2, f32[2,32,64]{2,1,0:T(8,128)S(1)} %get-tuple-element.70, f32[2,32,64]{2,1,0:T(8,128)S(1)} %get-tuple-element.54, f32[2,32,64]{2,1,0:T(8,128)S(1)} %get-tuple-element.37, bf16[2,32,64,1]{2,1,0,3:T(8,128)(2,1)S(1)} %get-tuple-element.64), kind=kOutput, calls=%fused_computation.23 | convolution fusion | flops 3932160 | bytes 1122304 | tf_op jit(solution)/shard_map/...hi,...hij->...hj/dot_general | solution.py:104
  162.8 3.5 %fusion.17 = f32[2,32,1,64]{3,2,1,0:T(1,128)S(1)} fusion(f32[2,32,64,64]{3,2,1,0:T(8,128)S(1)} %copy-done.2, f32[2,32,64]{2,1,0:T(8,128)S(1)} %get-tuple-element.68, f32[2,32,64]{2,1,0:T(8,128)S(1)} %get-tuple-element.56, f32[2,32,64]{2,1,0:T(8,128)S(1)} %get-tuple-element.52, f32[2,32,64]{2,1,0:T(8,128)S(1)} %get-tuple-element.70, ...), kind=kOutput, calls=%fused_computation.26 | convolution fusion | flops 4718592 | bytes 1171456 | tf_op jit(solution)/shard_map/...hi,...hij->...hj/dot_general | solution.py:104
  166.3 5.3 %fusion.11 = f32[2,32,1,64]{3,2,1,0:T(1,128)S(1)} fusion(f32[2,32,64,64]{3,2,1,0:T(8,128)S(1)} %copy-done.2, f32[2,32,64]{2,1,0:T(8,128)S(1)} %get-tuple-element.69, f32[2,32,64]{2,1,0:T(8,128)S(1)} %get-tuple-element.57, f32[2,32,64]{2,1,0:T(8,128)S(1)} %get-tuple-element.38, f32[2,32,64]{2,1,0:T(8,128)S(1)} %get-tuple-element.68, ...), kind=kOutput, calls=%fused_computation.17 | convolution fusion | flops 5505024 | bytes 1220608 | tf_op jit(solution)/shard_map/...hi,...hij->...hj/dot_general | solution.py:104
  173.0 0.7 fusion.81
  (77 shorter events, 3.3 us)
Async XLA Ops:
  6.5 92.3 %copy-start = (bf16[4096,192]{0,1:T(8,128)(2,1)S(1)}, bf16[4096,192]{0,1:T(8,128)(2,1)}, u32[]{:S(2)}) copy-start(bf16[4096,192]{0,1:T(8,128)(2,1)} %param.25) | copy-start | bytes 4718596
  6.5 90.7 %all-gather.2.cloned.1.call-start = ((), (), s32[]{:S(2)}) async-start(), calls=%async_computation.2 | async-start | bytes 1179648 | tf_op jit(solution)/shard_map/all_gather | solution.py:158
  8.2 46.8 %copy-start.14 = (s32[1,8]{1,0:T(1,128)S(1)}, s32[1,8]{1,0:T(1,128)}, u32[]{:S(2)}) copy-start(s32[1,8]{1,0:T(1,128)} %param.21) | copy-start | bytes 100
  8.2 46.9 %copy-start.6 = (f32[3,4096]{1,0:T(4,128)S(1)}, f32[3,4096]{1,0:T(4,128)}, u32[]{:S(2)}) copy-start(f32[3,4096]{1,0:T(4,128)} %param.24) | copy-start | bytes 147460
  52.2 46.6 %copy-start.15 = (f32[4096]{0:T(1024)S(1)}, f32[4096]{0:T(1024)}, u32[]{:S(2)}) copy-start(f32[4096]{0:T(1024)} %param.23) | copy-start | bytes 49156
  97.2 1.6 copy-start.3
  98.8 1.0 copy-start.4
  99.8 2.7 %copy-start.5 = (bf16[128,512]{1,0:T(8,128)(2,1)S(1)}, bf16[128,512]{1,0:T(8,128)(2,1)}, u32[]{:S(2)}) copy-start(bf16[128,512]{1,0:T(8,128)(2,1)} %param.29) | copy-start | bytes 393220
  99.8 2.7 %copy-start.13 = (f32[512]{0:T(512)S(1)}, f32[512]{0:T(512)}, u32[]{:S(2)}) copy-start(f32[512]{0:T(512)} %param.27) | copy-start | bytes 6148
  116.1 6.7 %copy-start.7 = (bf16[2,1,4,2048]{3,2,1,0:T(4,128)(2,1)S(1)}, bf16[2,1,4,2048]{3,2,1,0:T(4,128)(2,1)}, u32[]{:S(2)}) copy-start(bf16[2,1,4,2048]{3,2,1,0:T(4,128)(2,1)} %param.37) | copy-start | bytes 98308
  116.1 6.8 %copy-start.8 = (bf16[2,1,4,2048]{3,2,1,0:T(4,128)(2,1)S(1)}, bf16[2,1,4,2048]{3,2,1,0:T(4,128)(2,1)}, u32[]{:S(2)}) copy-start(bf16[2,1,4,2048]{3,2,1,0:T(4,128)(2,1)} %param.38) | copy-start | bytes 98308
  116.1 7.0 %copy-start.9 = (bf16[2,1,4,2048]{3,2,1,0:T(4,128)(2,1)S(1)}, bf16[2,1,4,2048]{3,2,1,0:T(4,128)(2,1)}, u32[]{:S(2)}) copy-start(bf16[2,1,4,2048]{3,2,1,0:T(4,128)(2,1)} %param.36) | copy-start | bytes 98308
  119.1 4.2 %copy-start.10 = (bf16[2,1,4,2048]{3,2,1,0:T(4,128)(2,1)S(1)}, bf16[2,1,4,2048]{3,2,1,0:T(4,128)(2,1)}, u32[]{:S(2)}) copy-start(bf16[2,1,4,2048]{3,2,1,0:T(4,128)(2,1)} %param.35) | copy-start | bytes 98308
  119.1 4.3 %copy-start.12 = (f32[64,64]{1,0:T(8,128)S(1)}, f32[64,64]{1,0:T(8,128)}, u32[]{:S(2)}) copy-start(f32[64,64]{1,0:T(8,128)} %param.32) | copy-start | bytes 49156
  119.1 28.4 %all-to-all-start = ((f32[1,8,8,4096]{3,2,0,1:T(8,128)}), f32[1,8,8,4096]{3,2,0,1:T(8,128)S(1)}, u32[]{:S(2)}, u32[]{:S(2)}) async-start(f32[1,8,8,4096]{3,2,0,1:T(8,128)} %bitcast.13), calls=%async_computation | async-start | bytes 2097152 | tf_op jit(solution)/shard_map/all_to_all | solution.py:192
  158.0 2.8 %copy-start.2 = (f32[2,32,64,64]{3,2,1,0:T(8,128)S(1)}, f32[2,32,64,64]{3,2,1,0:T(8,128)}, u32[]{:S(2)}) copy-start(f32[2,32,64,64]{3,2,1,0:T(8,128)} %reshape.536) | copy-start | bytes 3145732
  166.3 6.7 %copy-start.11 = (bf16[2,1,4,2048]{3,2,1,0:T(4,128)(2,1)S(1)}, bf16[2,1,4,2048]{3,2,1,0:T(4,128)(2,1)}, u32[]{:S(2)}) copy-start(bf16[2,1,4,2048]{3,2,1,0:T(4,128)(2,1)} %param.39) | copy-start | bytes 98308
  166.3 6.7 %dynamic-slice-start = ((f32[4096]{0:T(1024)}, s32[]{:T(128)}), f32[2048]{0:T(1024)S(1)}, s32[]{:S(2)}) async-start(f32[4096]{0:T(1024)} %param.33, s32[]{:T(128)} %select_n.43), calls=%async_computation.3 | async-start | bytes 16896 | tf_op jit(solution)/shard_map/dynamic_slice | solution.py:209
  166.3 6.6 %dynamic-slice-start.1 = ((f32[4096]{0:T(1024)}, s32[]{:T(128)}), f32[2048]{0:T(1024)S(1)}, s32[]{:S(2)}) async-start(f32[4096]{0:T(1024)} %param.34, s32[]{:T(128)} %select_n.43), calls=%async_computation.4 | async-start | bytes 16896 | tf_op jit(solution)/shard_map/dynamic_slice | solution.py:215
  166.3 7.4 %copy-start.1 = (bf16[4096,192]{0,1:T(8,128)(2,1)S(1)}, bf16[4096,192]{0,1:T(8,128)(2,1)}, u32[]{:S(2)}) copy-start(bf16[4096,192]{0,1:T(8,128)(2,1)} %param.25) | copy-start | bytes 4718596
Sparse Core Ops, SparseCore 0:
  55.1 42.1 all-gather.1
where the time goes:
time: 182 us; the launch traced here: 181 us
  waiting for transfers between devices  66 us (36%)
  local copies, waits for them, and re-layouts  57.7 us (32%)
  matrix products  29.8 us (16%)
  between operations  13.8 us (8%)
  other arithmetic  4.89 us (3%)
  blocking collectives  4.58 us (3%)
  starting transfers between devices  3.75 us (2%)
    unnamed x33, local copies, waits for them, and re-layouts  44.4 us
    all_gather x1, waiting for transfers between devices, per_device(): gathered = lax.all_gather(picked, 'wide', axis=0, tiled=True).T  42.1 us
    all_to_all x1, waiting for transfers between devices, per_device(): lax.all_to_all(recurrent_memories.reshape(1, bank_rows, head_local, atten...  23.9 us
    dot_general x4, matrix products, generation_iterations(): jnp.einsum('...hi,...hij->...hj', present_acceptance, recurrent_memories,...  13.7 us
    dot_general x1, matrix products, mix_project(): jnp.dot(branches[1], address_projector.T, preferred_element_type=jnp.floa...  4.66 us
    dot_general x1, matrix products, mix_project(): jnp.dot(branches[2], payload_projector.T, preferred_element_type=jnp.floa...  4.66 us
    all_to_all x1, blocking collectives, per_device(): lax.all_to_all(lax.all_to_all(recurrent_memories.reshape(1, bank_rows, he...  4.58 us
    all_to_all x1, starting transfers between devices, per_device(): lax.all_to_all(recurrent_memories.reshape(1, bank_rows, head_local, atten...  3.75 us
  transfers between devices with their start and end apart: 2, of which 2 were waited for; matrix products, arithmetic and copies ran while one was open for 0% of the time, Pallas kernels for 0%

commit v1 on v0

--- a/solution.py
+++ b/solution.py
@@ -4,6 +4,9 @@
 from jax.sharding import PartitionSpec as P
 
 norm_eps = 0.00064
+scan_heaps_here = lambda view, axis_tag: jnp.concatenate(
+    lax.all_to_all(jnp.stack(jnp.split(view, lax.axis_size(axis_tag), 1)), axis_tag, 0, 0), 2
+)
 
 
 def mix_project(
@@ -189,12 +192,9 @@
         bank_rows, head_local, attender_width, attender_width
     )
     handed = lax.all_to_all(
-        lax.all_to_all(
+        scan_heaps_here(
             recurrent_memories.reshape(1, bank_rows, head_local, attender_width * attender_width),
             "wide",
-            split_axis=1,
-            concat_axis=2,
-            tiled=True,
         ),
         "narrow",
         split_axis=2,

time: 182 us -> 189 us (1.038)
  local copies, waits for them, and re-layouts: 57.7 us -> 63.3 us
    unnamed x33 -> x40, local copies, waits for them, and re-layouts: 44.4 us -> 49 us
    reshape x0 -> x1, local copies, waits for them, and re-layouts: none -> 2.21 us  [jnp.concatenate(lax.all_to_all(jnp.stack(jnp.split(view, lax.axis_size(ax...]
where the time goes in v1:
time: 189 us; the launch traced here: 187 us
  waiting for transfers between devices  66 us (35%)
  local copies, waits for them, and re-layouts  63.3 us (33%)
  matrix products  29.8 us (16%)
  between operations  13.8 us (7%)
  blocking collectives  5.68 us (3%)
  other arithmetic  4.89 us (3%)
  starting transfers between devices  3.62 us (2%)
    unnamed x40, local copies, waits for them, and re-layouts  49 us
    all_gather x1, waiting for transfers between devices, per_device(): gathered = lax.all_gather(picked, 'wide', axis=0, tiled=True).T  42.1 us
    all_to_all x1, waiting for transfers between devices, lax.all_to_all(jnp.stack(jnp.split(view, lax.axis_size(axis_tag), 1)), ax...  23.9 us
    dot_general x4, matrix products, generation_iterations(): jnp.einsum('...hi,...hij->...hj', present_acceptance, recurrent_memories,...  13.7 us
    all_to_all x1, blocking collectives, per_device(): lax.all_to_all(scan_heaps_here(recurrent_memories.reshape(1, bank_rows, h...  5.68 us
    dot_general x1, matrix products, mix_project(): jnp.dot(branches[1], address_projector.T, preferred_element_type=jnp.floa...  4.66 us
    dot_general x1, matrix products, mix_project(): jnp.dot(branches[2], payload_projector.T, preferred_element_type=jnp.floa...  4.66 us
  transfers between devices with their start and end apart: 2, of which 2 were waited for; matrix products, arithmetic and copies ran while one was open for 0% of the time, Pallas kernels for 0%

profile of v1, /device:TPU:0, one launch (start us, length us, event | category | flops | bytes accessed | tf_op | source)
XLA Modules:
  0.0 187.2 jit_solution(10193676445742396559)
XLA Ops:
  6.5 0.9 reshape.534
  7.4 0.8 reshape.533
  8.2 44.0 %copy.68 = bf16[512,32768]{0,1:T(8,128)(2,1)} copy(bf16[512,32768]{1,0:T(8,128)(2,1)} %param.22) | data formatting | bytes 67108864 | tf_op args[2]
  52.2 2.0 %gather_fusion = bf16[128,512]{1,0:T(8,128)(2,1)S(1)} fusion(bf16[512,32768]{0,1:T(8,128)(2,1)} %copy.68, s32[1024]{0:T(1024)S(1)} %pad_clamp_fusion), kind=kCustom, calls=%fused_computation | custom fusion | bytes 262656 | tf_op jit(solution)/shard_map/jit(_take)/gather | solution.py:160
  54.2 0.7 select_bitcast_fusion
  55.1 42.1 %all-gather.2.cloned.1.call-done = bf16[4096,128]{0,1:T(8,128)(2,1)} async-done(((bf16[512,128]{0,1:T(8,128)(2,1)}), bf16[4096,128]{0,1:T(8,128)(2,1)}) %all-gather.2.cloned.1.call-update) | async-done | bytes 1048592 | tf_op jit(solution)/shard_map/all_gather | solution.py:161
  97.2 1.6 pad_slice_fusion
  98.8 0.7 fusion.20
  99.8 2.7 %fusion.22 = bf16[128,128]{1,0:T(8,128)(2,1)S(1)} fusion(bf16[4096,128]{1,0:T(8,128)(2,1)} %param.28, bf16[128,4096]{1,0:T(8,128)(2,1)} %bitcast.212, bf16[4096,128]{0,1:T(8,128)(2,1)S(1)} %copy-done.3, f32[4096]{0:T(1024)S(1)} %bitcast.230, bf16[3,64,4096]{2,1,0:T(8,128)(2,1)} %param.26, bf16[128,192]{0,1:T(8,128)(2,1)S(1)} %fusion.20), kind=kOutput, calls=%fused_computation.35 | convolution fusion | flops 205012992 | bytes 3735552 | tf_op jit(solution)/shard_map/while/body/eval_jaxpr/dot_general | solution.py:46
  103.1 4.7 %convolution_convert_fusion = bf16[128,512]{1,0:T(8,128)(2,1)S(1)} fusion(bf16[512,4096]{1,0:T(8,128)(2,1)} %param.31, bf16[128,4096]{1,0:T(8,128)(2,1)} %bitcast.213, bf16[4096,128]{0,1:T(8,128)(2,1)S(1)} %copy-done.3, f32[4096]{0:T(1024)S(1)} %bitcast.229, bf16[3,64,4096]{2,1,0:T(8,128)(2,1)} %param.26, bf16[128,192]{0,1:T(8,128)(2,1)S(1)} %fusion.20), kind=kOutput, calls=%fused_computation.29 | convolution fusion | flops 607715328 | bytes 6979584 | tf_op jit(solution)/shard_map/while/body/eval_jaxpr/dot_general | solution.py:54
  108.0 4.7 %fusion.19 = f32[128,512]{1,0:T(8,128)S(1)} fusion(bf16[512,4096]{1,0:T(8,128)(2,1)} %param.30, bf16[128,4096]{1,0:T(8,128)(2,1)} %bitcast.214, bf16[4096,128]{0,1:T(8,128)(2,1)S(1)} %copy-done.3, f32[4096]{0:T(1024)S(1)} %bitcast.228, bf16[3,64,4096]{2,1,0:T(8,128)(2,1)} %param.26, bf16[128,192]{0,1:T(8,128)(2,1)S(1)} %fusion.20), kind=kOutput, calls=%fused_computation.31 | convolution fusion | flops 607780864 | bytes 7110656 | tf_op jit(solution)/shard_map/while/body/eval_jaxpr/dot_general | solution.py:51
  112.8 3.3 %fusion.56 = f32[8,8,64,64]{3,2,1,0:T(8,128)} fusion(f32[8,16,8,64]{3,2,1,0:T(8,128)S(1)} %reshape.550, f32[8,16,8,64]{3,2,0,1:T(8,128)S(1)} %reduce_window_sum.15, bf16[8,16,8,64]{3,2,1,0:T(8,128)(2,1)S(1)} %reshape.535, f32[8,8,64]{2,1,0:T(8,128)S(1)} %sub.51, pred[8,16]{1,0:T(8,128)(4,1)S(1)} %copy.69), kind=kOutput, calls=%fused_computation.66 | convolution fusion | flops 50593792 | bytes 1720448 | tf_op jit(solution)/shard_map/while/body/eval_jaxpr/rlhi,rlhj->rhij/dot_general | solution.py:75
  116.1 2.1 %reshape_reshape.3 = f32[1,8,8,4096]{3,2,1,0:T(8,128)S(1)} reshape(f32[8,8,64,64]{3,2,1,0:T(8,128)} %fusion.56) | data formatting | bytes 2097152 | tf_op jit(solution)/shard_map/reshape;reshape | solution.py:196
  123.6 3.6 %all-to-all-start = ((f32[8,1,1,8,4096]{4,3,2,1,0:T(8,128)}), f32[8,1,1,8,4096]{4,3,2,1,0:T(8,128)S(1)}, u32[]{:S(2)}, u32[]{:S(2)}) async-start(f32[8,1,1,8,4096]{4,3,2,1,0:T(8,128)} %fusion.72), calls=%async_computation | async-start | bytes 2097152 | tf_op jit(solution)/shard_map/all_to_all | solution.py:8
  127.9 23.9 %all-to-all-done = f32[8,1,1,8,4096]{4,3,2,1,0:T(8,128)S(1)} async-done(((f32[8,1,1,8,4096]{4,3,2,1,0:T(8,128)}), f32[8,1,1,8,4096]{4,3,2,1,0:T(8,128)S(1)}, u32[]{:S(2)}, u32[]{:S(2)}) %all-to-all-start) | async-done | bytes 1048608 | tf_op jit(solution)/shard_map/all_to_all | solution.py:8
  151.9 2.2 %reshape.536 = f32[1,1,64,4096]{3,1,0,2:T(1,128)} reshape(f32[8,1,1,8,4096]{4,3,2,1,0:T(8,128)S(1)} %all-to-all-done) | data formatting | bytes 2097152 | tf_op jit(solution)/shard_map/reshape | solution.py:7
  154.1 5.7 %all_to_all.14 = f32[1,1,64,4096]{3,1,0,2:T(1,128)S(1)} all-to-all(f32[1,1,64,4096]{3,1,0,2:T(1,128)} %reshape.536), channel_id=1, replica_groups=mesh['groups'=2,'wide'=8,'narrow'=2] {'narrow'}, dimensions={2} | all-to-all | bytes 2097152 | tf_op jit(solution)/shard_map/all_to_all | solution.py:194
  159.8 2.6 %reduce.6 = f32[64,4096]{1,0:T(8,128)S(1)} reduce(f32[1,1,64,4096]{3,1,0,2:T(1,128)S(1)} %all_to_all.14, f32[]{:T(128)} %constant.68), dimensions={0,1}, to_apply=%all_to_all.5.reduce_sub_computation | reduce | bytes 2097156 | tf_op jit(solution)/shard_map/all_to_all | solution.py:194
  162.4 2.2 %reshape.537 = f32[2,32,64,64]{3,2,1,0:T(8,128)} reshape(f32[64,4096]{1,0:T(8,128)S(1)} %reduce.6) | data formatting | bytes 2097152 | tf_op jit(solution)/shard_map/reshape.33
  164.6 2.8 %fusion.107 = f32[2,32,1,64]{3,2,1,0:T(1,128)S(1)} fusion(f32[2,32,64,64]{3,2,1,0:T(8,128)} %reshape.537, bf16[2,32,64,1]{2,1,0,3:T(8,128)(2,1)S(1)} %get-tuple-element.61), kind=kOutput, calls=%fused_computation.143 | convolution fusion | flops 3145728 | bytes 1073152 | tf_op jit(solution)/shard_map/...hi,...hij->...hj/dot_general | solution.py:107
  167.4 2.0 %fusion.15 = f32[2,32,1,64]{3,2,1,0:T(1,128)S(1)} fusion(f32[2,32,64,64]{3,2,1,0:T(8,128)S(1)} %copy-done.2, f32[2,32,64]{2,1,0:T(8,128)S(1)} %get-tuple-element.70, f32[2,32,64]{2,1,0:T(8,128)S(1)} %get-tuple-element.54, f32[2,32,64]{2,1,0:T(8,128)S(1)} %get-tuple-element.37, bf16[2,32,64,1]{2,1,0,3:T(8,128)(2,1)S(1)} %get-tuple-element.64), kind=kOutput, calls=%fused_computation.23 | convolution fusion | flops 3932160 | bytes 1122304 | tf_op jit(solution)/shard_map/...hi,...hij->...hj/dot_general | solution.py:107
  169.4 3.5 %fusion.17 = f32[2,32,1,64]{3,2,1,0:T(1,128)S(1)} fusion(f32[2,32,64,64]{3,2,1,0:T(8,128)S(1)} %copy-done.2, f32[2,32,64]{2,1,0:T(8,128)S(1)} %get-tuple-element.68, f32[2,32,64]{2,1,0:T(8,128)S(1)} %get-tuple-element.56, f32[2,32,64]{2,1,0:T(8,128)S(1)} %get-tuple-element.52, f32[2,32,64]{2,1,0:T(8,128)S(1)} %get-tuple-element.70, ...), kind=kOutput, calls=%fused_computation.26 | convolution fusion | flops 4718592 | bytes 1171456 | tf_op jit(solution)/shard_map/...hi,...hij->...hj/dot_general | solution.py:107
  172.9 5.3 %fusion.11 = f32[2,32,1,64]{3,2,1,0:T(1,128)S(1)} fusion(f32[2,32,64,64]{3,2,1,0:T(8,128)S(1)} %copy-done.2, f32[2,32,64]{2,1,0:T(8,128)S(1)} %get-tuple-element.69, f32[2,32,64]{2,1,0:T(8,128)S(1)} %get-tuple-element.57, f32[2,32,64]{2,1,0:T(8,128)S(1)} %get-tuple-element.38, f32[2,32,64]{2,1,0:T(8,128)S(1)} %get-tuple-element.68, ...), kind=kOutput, calls=%fused_computation.17 | convolution fusion | flops 5505024 | bytes 1220608 | tf_op jit(solution)/shard_map/...hi,...hij->...hj/dot_general | solution.py:107
  179.6 0.7 fusion.89
  (85 shorter events, 8.6 us)
Async XLA Ops:
  6.5 92.3 %copy-start = (bf16[4096,192]{0,1:T(8,128)(2,1)S(1)}, bf16[4096,192]{0,1:T(8,128)(2,1)}, u32[]{:S(2)}) copy-start(bf16[4096,192]{0,1:T(8,128)(2,1)} %param.25) | copy-start | bytes 4718596
  6.5 90.7 %all-gather.2.cloned.1.call-start = ((), (), s32[]{:S(2)}) async-start(), calls=%async_computation.2 | async-start | bytes 1179648 | tf_op jit(solution)/shard_map/all_gather | solution.py:161
  8.2 46.8 %copy-start.14 = (s32[1,8]{1,0:T(1,128)S(1)}, s32[1,8]{1,0:T(1,128)}, u32[]{:S(2)}) copy-start(s32[1,8]{1,0:T(1,128)} %param.21) | copy-start | bytes 100
  8.2 46.9 %copy-start.6 = (f32[3,4096]{1,0:T(4,128)S(1)}, f32[3,4096]{1,0:T(4,128)}, u32[]{:S(2)}) copy-start(f32[3,4096]{1,0:T(4,128)} %param.24) | copy-start | bytes 147460
  52.2 46.6 %copy-start.15 = (f32[4096]{0:T(1024)S(1)}, f32[4096]{0:T(1024)}, u32[]{:S(2)}) copy-start(f32[4096]{0:T(1024)} %param.23) | copy-start | bytes 49156
  97.2 1.6 copy-start.3
  98.8 1.0 copy-start.4
  99.8 2.7 %copy-start.5 = (bf16[128,512]{1,0:T(8,128)(2,1)S(1)}, bf16[128,512]{1,0:T(8,128)(2,1)}, u32[]{:S(2)}) copy-start(bf16[128,512]{1,0:T(8,128)(2,1)} %param.29) | copy-start | bytes 393220
  99.8 2.7 %copy-start.13 = (f32[512]{0:T(512)S(1)}, f32[512]{0:T(512)}, u32[]{:S(2)}) copy-start(f32[512]{0:T(512)} %param.27) | copy-start | bytes 6148
  118.3 8.9 %copy-start.7 = (bf16[2,1,4,2048]{3,2,1,0:T(4,128)(2,1)S(1)}, bf16[2,1,4,2048]{3,2,1,0:T(4,128)(2,1)}, u32[]{:S(2)}) copy-start(bf16[2,1,4,2048]{3,2,1,0:T(4,128)(2,1)} %param.37) | copy-start | bytes 98308
  118.9 8.4 %copy-start.8 = (bf16[2,1,4,2048]{3,2,1,0:T(4,128)(2,1)S(1)}, bf16[2,1,4,2048]{3,2,1,0:T(4,128)(2,1)}, u32[]{:S(2)}) copy-start(bf16[2,1,4,2048]{3,2,1,0:T(4,128)(2,1)} %param.38) | copy-start | bytes 98308
  119.6 7.9 %copy-start.9 = (bf16[2,1,4,2048]{3,2,1,0:T(4,128)(2,1)S(1)}, bf16[2,1,4,2048]{3,2,1,0:T(4,128)(2,1)}, u32[]{:S(2)}) copy-start(bf16[2,1,4,2048]{3,2,1,0:T(4,128)(2,1)} %param.36) | copy-start | bytes 98308
  119.6 8.0 %copy-start.10 = (bf16[2,1,4,2048]{3,2,1,0:T(4,128)(2,1)S(1)}, bf16[2,1,4,2048]{3,2,1,0:T(4,128)(2,1)}, u32[]{:S(2)}) copy-start(bf16[2,1,4,2048]{3,2,1,0:T(4,128)(2,1)} %param.35) | copy-start | bytes 98308
  120.3 7.4 %copy-start.12 = (f32[64,64]{1,0:T(8,128)S(1)}, f32[64,64]{1,0:T(8,128)}, u32[]{:S(2)}) copy-start(f32[64,64]{1,0:T(8,128)} %param.32) | copy-start | bytes 49156
  123.6 28.3 %all-to-all-start = ((f32[8,1,1,8,4096]{4,3,2,1,0:T(8,128)}), f32[8,1,1,8,4096]{4,3,2,1,0:T(8,128)S(1)}, u32[]{:S(2)}, u32[]{:S(2)}) async-start(f32[8,1,1,8,4096]{4,3,2,1,0:T(8,128)} %fusion.72), calls=%async_computation | async-start | bytes 2097152 | tf_op jit(solution)/shard_map/all_to_all | solution.py:8
  164.6 2.8 %copy-start.2 = (f32[2,32,64,64]{3,2,1,0:T(8,128)S(1)}, f32[2,32,64,64]{3,2,1,0:T(8,128)}, u32[]{:S(2)}) copy-start(f32[2,32,64,64]{3,2,1,0:T(8,128)} %reshape.537) | copy-start | bytes 3145732
  172.9 6.7 %copy-start.11 = (bf16[2,1,4,2048]{3,2,1,0:T(4,128)(2,1)S(1)}, bf16[2,1,4,2048]{3,2,1,0:T(4,128)(2,1)}, u32[]{:S(2)}) copy-start(bf16[2,1,4,2048]{3,2,1,0:T(4,128)(2,1)} %param.39) | copy-start | bytes 98308
  172.9 6.7 %dynamic-slice-start = ((f32[4096]{0:T(1024)}, s32[]{:T(128)}), f32[2048]{0:T(1024)S(1)}, s32[]{:S(2)}) async-start(f32[4096]{0:T(1024)} %param.33, s32[]{:T(128)} %select_n.43), calls=%async_computation.3 | async-start | bytes 16896 | tf_op jit(solution)/shard_map/dynamic_slice | solution.py:209
  172.9 6.6 %dynamic-slice-start.1 = ((f32[4096]{0:T(1024)}, s32[]{:T(128)}), f32[2048]{0:T(1024)S(1)}, s32[]{:S(2)}) async-start(f32[4096]{0:T(1024)} %param.34, s32[]{:T(128)} %select_n.43), calls=%async_computation.4 | async-start | bytes 16896 | tf_op jit(solution)/shard_map/dynamic_slice | solution.py:215
  172.9 7.4 %copy-start.1 = (bf16[4096,192]{0,1:T(8,128)(2,1)S(1)}, bf16[4096,192]{0,1:T(8,128)(2,1)}, u32[]{:S(2)}) copy-start(bf16[4096,192]{0,1:T(8,128)(2,1)} %param.25) | copy-start | bytes 4718596
Sparse Core Ops, SparseCore 0:
  55.1 42.1 all-gather.1
